TPU v7x, 32 devices: a whole 2x2x4 slice. The times are simulated.
32 devices in a mesh: groups: 2 (over y), shard: 2 (over x), expert: 4 (over z), section: 2 (over core).
Axes of the slice: x: 2, y: 2, z: 4, core: 2. Of those that a mesh axis runs over, the one named last changes fastest.
Arguments:
- tokens: bfloat16 [2, 512, 6144], P(None, ('groups', 'shard', 'expert')), parts along dimension 1, may hold values from -6 to 6
- norm_gain: float32 [2, 6144], P('section'), may hold values from 0.5 to 2
- route_ids: int32 [2, 2, 512, 2], P('section', None, ('groups', 'shard', 'expert')), parts along dimension 2, may hold values from 0 to 3, all different within a row; in each aligned block of 32 rows (0 to 31, 32 to 63, ..., all dimensions but the last counted through in order) at most 18 rows name the same one
- route_weights: float32 [2, 2, 512, 2], P('section', None, ('groups', 'shard', 'expert')), parts along dimension 2, may hold values from 0.25 to 1
- gate_blocks: bfloat16 [2, 4, 64, 1, 128, 128], P('section', 'expert', 'shard'), may hold values from -0.5 to 0.5
- up_blocks: bfloat16 [2, 4, 64, 1, 128, 128], P('section', 'expert', 'shard'), may hold values from -0.5 to 0.5
- down_blocks: bfloat16 [2, 4, 64, 1, 128, 128], P('section', 'expert', 'shard'), may hold values from -0.4375 to 0.4375
- gate_rows: int32 [2, 4, 64, 1], P('section', 'expert', 'shard'), may hold values from 0 to 47
- down_cols: int32 [2, 4, 64, 1], P('section', 'expert', 'shard'), may hold values from 0 to 47
Outputs:
- hidden_states: bfloat16 [2, 2, 512, 6144], P('section', None, ('groups', 'shard', 'expert')), parts along dimension 2
There are 2 independent parts, one for each index of `groups`. A program takes and returns all parts, laid end to end along the dimension named above; an argument that names none is the same for every part. Nothing has to cross between parts.
Inputs may be any that keep to these rules, and one draw needn't show every extreme that they name: `route_ids`: the 2 experts of a token differ; among the 32 tokens of one device, one micro-batch and one layer, no expert is named by more than 18 tokens, a bound that some block reaches of them.
All inputs are finite; a program needn't handle non-finite values.
Results may differ from a plain program's by a relative error of at most 0.0064.
Values may be sent and summed in bfloat16 or wider, within the bound.
A program may use at most 64 MiB of HBM per device.

v0:
```python
import jax
import jax.numpy as jnp
from jax import lax
from jax.sharding import PartitionSpec as P

TOP = 2


def passed_along(shard, axis, by):
    length = lax.axis_size(axis)
    pairs = [(i, i + by) for i in range(length) if 0 <= i + by < length]
    return lax.ppermute(shard, axis, pairs)


def normalize(values, gain_row):
    wide = values.astype(jnp.float32)
    scale = lax.rsqrt(jnp.mean(wide * wide, axis=-1, keepdims=True) + 1e-05)
    return (wide * scale * gain_row).astype(jnp.bfloat16)


def hidden_part(inputs, gate_w, up_w, down_w, row_index, col_index):
    row_total = inputs.shape[0]
    block_size = gate_w.shape[-1]
    block_rows = inputs.shape[1] // block_size
    blocks = inputs.reshape(row_total, block_rows, block_size)
    picked = jnp.take(blocks, row_index.reshape(-1), axis=1)
    picked = picked.reshape(row_total, row_index.shape[0], row_index.shape[1], block_size)
    gate = jnp.einsum("rckd,ckdf->rcf", picked, gate_w, preferred_element_type=jnp.float32)
    up_val = jnp.einsum("rckd,ckdf->rcf", picked, up_w, preferred_element_type=jnp.float32)
    hidden = (jax.nn.silu(gate) * up_val).astype(jnp.bfloat16)
    columns = jnp.arange(block_rows, dtype=jnp.int32)
    part_out = jnp.einsum("rcf,cfo->rco", hidden, down_w[:, 0], preferred_element_type=jnp.float32)
    destinations = (col_index[:, 0][:, None] == columns[None, :]).astype(jnp.float32)
    result = jnp.einsum("rco,cj->rjo", part_out, destinations, precision=lax.Precision.HIGHEST)
    return result


def body(
    tokens,
    norm_gain,
    route_ids,
    route_weights,
    gate_blocks,
    up_blocks,
    down_blocks,
    gate_rows,
    down_cols,
):
    experts_here = gate_blocks.shape[1]
    group_count = lax.axis_size("expert")
    expert_total = group_count * experts_here
    micro_count, row_count, model_width = tokens.shape
    capacity = min(row_count, max(row_count * 9 // 16, row_count * TOP // expert_total + 2))
    section_index = lax.axis_index("section")
    gain_row = norm_gain[0]
    local_blocks = (gate_blocks[0], up_blocks[0], down_blocks[0], gate_rows[0], down_cols[0])
    gathered = (
        lax.all_gather(local_blocks[0], "shard", axis=1, tiled=True),
        lax.all_gather(local_blocks[1], "shard", axis=1, tiled=True),
        lax.all_gather(local_blocks[2], "shard", axis=1, tiled=True),
        lax.all_gather(local_blocks[3], "shard", axis=1, tiled=True),
        lax.all_gather(local_blocks[4], "shard", axis=1, tiled=True),
    )
    handed = jnp.zeros((row_count, model_width), jnp.bfloat16)
    produced = []
    for tick in range(micro_count + 1):
        own_input = tokens[min(tick, micro_count - 1)]
        current = jnp.where(section_index == 0, own_input, handed)
        micro_index = jnp.clip(tick - section_index, 0, micro_count - 1)
        chosen_ids = lax.dynamic_index_in_dim(route_ids[0], micro_index, 0, keepdims=False)
        chosen_weights = lax.dynamic_index_in_dim(route_weights[0], micro_index, 0, keepdims=False)
        normed = normalize(current, gain_row)
        flat_ids = chosen_ids.reshape(-1)
        slot_count = flat_ids.shape[0]
        onehot = (flat_ids[:, None] == jnp.arange(expert_total, dtype=jnp.int32)[None, :]).astype(
            jnp.int32
        )
        before = jnp.cumsum(onehot, axis=0) - onehot
        target = flat_ids * capacity + jnp.sum(before * onehot, axis=1)
        matches = target[None, :] == jnp.arange(expert_total * capacity, dtype=jnp.int32)[:, None]
        filled = jnp.any(matches, axis=1)
        source = (
            jnp.sum(jnp.where(matches, jnp.arange(slot_count, dtype=jnp.int32)[None, :], 0), axis=1)
            // TOP
        )
        outgoing = jnp.where(filled[:, None], normed[source], jnp.zeros((), jnp.bfloat16))
        outgoing = outgoing.reshape(group_count, experts_here, capacity, model_width)
        arrived = lax.all_to_all(outgoing, "expert", split_axis=0, concat_axis=0, tiled=True)
        row_total = arrived.shape[0] * arrived.shape[2]
        inputs = arrived[:, 0].reshape(row_total, model_width)
        totals = hidden_part(
            inputs, gathered[0][0], gathered[1][0], gathered[2][0], gathered[3][0], gathered[4][0]
        )
        outputs = [
            totals.reshape(arrived.shape[0], arrived.shape[2], model_width).astype(jnp.bfloat16)
        ]
        returned = lax.all_to_all(
            jnp.stack(outputs, 1), "expert", split_axis=0, concat_axis=0, tiled=True
        )
        picked = returned.reshape(expert_total * capacity, model_width)[target].reshape(
            row_count, TOP, model_width
        )
        mixed_rows = current.astype(jnp.float32) + jnp.sum(
            chosen_weights[:, :, None] * picked.astype(jnp.float32), axis=1
        )
        result = mixed_rows.astype(jnp.bfloat16)
        produced.append(result)
        if tick < micro_count:
            handed = passed_along(result, "section", 1)
    finished = [
        jnp.where(section_index == 0, produced[index], produced[index + 1])
        for index in range(micro_count)
    ]
    return jnp.stack(finished, 0)[None]


def solution(mesh):
    in_specs = (
        P(None, ("groups", "shard", "expert"), None),
        P("section", None),
        P("section", None, ("groups", "shard", "expert"), None),
        P("section", None, ("groups", "shard", "expert"), None),
        P("section", "expert", "shard", None, None, None),
        P("section", "expert", "shard", None, None, None),
        P("section", "expert", "shard", None, None, None),
        P("section", "expert", "shard", None),
        P("section", "expert", "shard", None),
    )
    out_specs = P("section", None, ("groups", "shard", "expert"), None)
    return jax.shard_map(body, mesh=mesh, in_specs=in_specs, out_specs=out_specs, check_vma=False)
```

profile of v0, /device:TPU:17, one launch (start us, length us, event | category | flops | bytes accessed | tf_op | source)
XLA Modules:
  0.0 358.9 jit_solution(11724038737582841724)
XLA Ops:
  13.2 4.8 %all-to-all-start = ((bf16[4,1,18,6144]{3,2,1,0:T(8,128)(2,1)}), bf16[4,1,18,6144]{3,2,1,0:T(8,128)(2,1)S(1)}, u32[]{:S(2)}, u32[]{:S(2)}) async-start(bf16[4,1,18,6144]{3,2,1,0:T(8,128)(2,1)} %select_bitcast_fusion.2), calls=%async_computation | async-start | bytes 2359296 | tf_op jit(solution)/shard_map/all_to_all | solution.py:88
  19.3 3.7 %all-reduce.2 = (s32[64]{0:T(128)S(1)}, s32[64]{0:T(128)S(1)}) all-reduce(s32[64]{0:T(128)S(1)} %bitcast_dynamic-update-slice_fusion, s32[64]{0:T(128)S(1)} %bitcast_dynamic-update-slice_fusion.1), channel_id=3, replica_groups=mesh['groups'=2,'shard'=2,'expert'=4,'section'=2] {'shard'}, use_global_device_ids=true, to_apply=%add.1 | all-reduce | flops 128 | bytes 1024 | tf_op jit(solution)/shard_map/reshape;squeeze | solution.py:26
  23.1 20.0 %all-to-all-done = bf16[4,1,18,6144]{3,2,1,0:T(8,128)(2,1)S(1)} async-done(((bf16[4,1,18,6144]{3,2,1,0:T(8,128)(2,1)}), bf16[4,1,18,6144]{3,2,1,0:T(8,128)(2,1)S(1)}, u32[]{:S(2)}, u32[]{:S(2)}) %all-to-all-start) | async-done | bytes 884768 | tf_op jit(solution)/shard_map/all_to_all | solution.py:88
  44.7 3.8 %fusion.28 = f32[64,72,128]{2,1,0:T(8,128)} fusion(bf16[1,1,64,1,128,128]{5,4,3,1,0,2:T(8,128)(2,1)} %all-gather.11.cloned.1.call-done, bf16[64,72,128]{2,1,0:T(8,128)(2,1)S(1)} %gather_fusion.6, pred[64]{0:T(512)(128)(4,1)S(1)} %compare_and_fusion), kind=kOutput, calls=%fused_computation.46 | convolution fusion | flops 151584768 | bytes 5636160 | tf_op jit(solution)/shard_map/rckd,ckdf->rcf/dot_general | solution.py:29
  48.5 29.2 %all-gather.13.cloned.1.call-done = bf16[1,1,64,1,128,128]{5,4,3,1,0,2:T(8,128)(2,1)} async-done(((bf16[1,1,32,1,128,128]{5,4,3,1,0,2:T(8,128)(2,1)}), bf16[1,1,64,1,128,128]{5,4,3,1,0,2:T(8,128)(2,1)}) %all-gather.13.cloned.1.call-update) | async-done | bytes 2097168 | tf_op jit(solution)/shard_map/all_gather | solution.py:60
  77.7 34.7 %all-gather.9.cloned.1.call-done = bf16[1,1,64,1,128,128]{5,4,3,1,0,2:T(8,128)(2,1)} async-done(((bf16[1,1,32,1,128,128]{5,4,3,1,0,2:T(8,128)(2,1)}), bf16[1,1,64,1,128,128]{5,4,3,1,0,2:T(8,128)(2,1)}) %all-gather.9.cloned.1.call-update) | async-done | bytes 2097168 | tf_op jit(solution)/shard_map/all_gather | solution.py:58
  112.4 5.8 %fusion.36 = f32[72,64,128]{2,0,1:T(8,128)} fusion(bf16[1,1,64,1,128,128]{5,4,3,1,0,2:T(8,128)(2,1)} %all-gather.13.cloned.1.call-done, f32[64,72,128]{2,1,0:T(8,128)} %fusion.28, bf16[1,1,64,1,128,128]{5,4,3,1,0,2:T(8,128)(2,1)} %all-gather.9.cloned.1.call-done, bf16[64,72,128]{2,1,0:T(8,128)(2,1)S(1)} %gather_fusion.6, pred[64]{0:T(512)(128)(4,1)S(1)} %compare_and_fusion), kind=kOutput, calls=%fused_computation.54 | convolution fusion | flops 306118656 | bytes 10092608 | tf_op jit(solution)/shard_map/rcf,cfo->rco/dot_general | solution.py:32
  118.2 3.1 fusion.72
  122.8 4.6 %all-to-all-start.1 = ((bf16[4,1,18,6144]{3,2,1,0:T(8,128)(2,1)}), bf16[4,1,18,6144]{3,2,1,0:T(8,128)(2,1)S(1)}, u32[]{:S(2)}, u32[]{:S(2)}) async-start(bf16[4,1,18,6144]{3,2,1,0:T(8,128)(2,1)} %bitcast.22), calls=%async_computation.1 | async-start | bytes 2359296 | tf_op jit(solution)/shard_map/all_to_all | solution.py:97
  129.6 22.8 %all-to-all-done.1 = bf16[4,1,18,6144]{3,2,1,0:T(8,128)(2,1)S(1)} async-done(((bf16[4,1,18,6144]{3,2,1,0:T(8,128)(2,1)}), bf16[4,1,18,6144]{3,2,1,0:T(8,128)(2,1)S(1)}, u32[]{:S(2)}, u32[]{:S(2)}) %all-to-all-start.1) | async-done | bytes 884768 | tf_op jit(solution)/shard_map/all_to_all | solution.py:97
  154.8 2.1 multiply_reduce_fusion.2
  158.4 2.5 collective-permute-done
  163.7 31.1 %all_to_all.30 = bf16[4,1,18,6144]{3,2,1,0:T(8,128)(2,1)S(1)} all-to-all(bf16[4,1,18,6144]{3,2,1,0:T(8,128)(2,1)S(1)} %select_bitcast_fusion.1), channel_id=1, replica_groups=mesh['groups'=2,'shard'=2,'expert'=4,'section'=2] {'expert'}, dimensions={0} | all-to-all | bytes 1769472 | tf_op jit(solution)/shard_map/all_to_all | solution.py:88
  197.8 1.9 gather_fusion.7
  199.6 3.6 %fusion.26 = f32[64,72,128]{2,1,0:T(8,128)} fusion(bf16[1,1,64,1,128,128]{5,4,3,1,0,2:T(8,128)(2,1)S(1)} %copy-done, bf16[64,72,128]{2,1,0:T(8,128)(2,1)} %gather_fusion.7, pred[64]{0:T(512)(128)(4,1)S(1)} %copy-done.18), kind=kOutput, calls=%fused_computation.44 | convolution fusion | flops 151584768 | bytes 5636160 | tf_op jit(solution)/shard_map/rckd,ckdf->rcf/dot_general | solution.py:29
  203.3 5.8 %fusion.39 = f32[72,64,128]{2,0,1:T(8,128)} fusion(bf16[1,1,64,1,128,128]{5,4,3,1,0,2:T(8,128)(2,1)} %all-gather.13.cloned.1.call-done, f32[64,72,128]{2,1,0:T(8,128)} %fusion.26, bf16[1,1,64,1,128,128]{5,4,3,1,0,2:T(8,128)(2,1)} %all-gather.9.cloned.1.call-done, bf16[64,72,128]{2,1,0:T(8,128)(2,1)S(1)} %copy-done.4, pred[64]{0:T(512)(128)(4,1)S(1)} %copy-done.18), kind=kOutput, calls=%fused_computation.55 | convolution fusion | flops 306118656 | bytes 10092608 | tf_op jit(solution)/shard_map/rcf,cfo->rco/dot_general | solution.py:32
  209.1 3.1 fusion.69
  213.7 7.1 %all-to-all-start.3 = ((bf16[4,1,18,6144]{3,2,1,0:T(8,128)(2,1)}), bf16[4,1,18,6144]{3,2,1,0:T(8,128)(2,1)}, u32[]{:S(2)}, u32[]{:S(2)}) async-start(bf16[4,1,18,6144]{3,2,1,0:T(8,128)(2,1)} %bitcast.35), calls=%async_computation.3 | async-start | bytes 2359296 | tf_op jit(solution)/shard_map/all_to_all | solution.py:97
  221.9 24.0 %all-to-all-done.3 = bf16[4,1,18,6144]{3,2,1,0:T(8,128)(2,1)} async-done(((bf16[4,1,18,6144]{3,2,1,0:T(8,128)(2,1)}), bf16[4,1,18,6144]{3,2,1,0:T(8,128)(2,1)}, u32[]{:S(2)}, u32[]{:S(2)}) %all-to-all-start.3) | async-done | bytes 884768 | tf_op jit(solution)/shard_map/all_to_all | solution.py:97
  247.5 1.9 gather_fusion.3
  249.4 3.0 reshape.505
  252.4 3.6 multiply_reduce_fusion.1
  258.3 2.5 collective-permute-done.1
  262.0 2.0 gather_fusion.4
  265.6 31.2 %all_to_all.31 = bf16[4,1,18,6144]{3,2,1,0:T(8,128)(2,1)S(1)} all-to-all(bf16[4,1,18,6144]{3,2,1,0:T(8,128)(2,1)S(1)} %select_bitcast_fusion), channel_id=1, replica_groups=mesh['groups'=2,'shard'=2,'expert'=4,'section'=2] {'expert'}, dimensions={0} | all-to-all | bytes 1769472 | tf_op jit(solution)/shard_map/all_to_all | solution.py:88
  299.6 1.9 gather_fusion.8
  301.4 3.6 %fusion.24 = f32[64,72,128]{2,1,0:T(8,128)} fusion(bf16[1,1,64,1,128,128]{5,4,3,1,0,2:T(8,128)(2,1)S(1)} %copy-done, bf16[64,72,128]{2,1,0:T(8,128)(2,1)} %gather_fusion.8, pred[64]{0:T(512)(128)(4,1)S(1)} %copy-done.18), kind=kOutput, calls=%fused_computation.42 | convolution fusion | flops 151584768 | bytes 5636160 | tf_op jit(solution)/shard_map/rckd,ckdf->rcf/dot_general | solution.py:29
  305.1 5.8 %fusion.42 = f32[72,64,128]{2,0,1:T(8,128)} fusion(bf16[1,1,64,1,128,128]{5,4,3,1,0,2:T(8,128)(2,1)} %all-gather.13.cloned.1.call-done, f32[64,72,128]{2,1,0:T(8,128)} %fusion.24, bf16[1,1,64,1,128,128]{5,4,3,1,0,2:T(8,128)(2,1)} %all-gather.9.cloned.1.call-done, bf16[64,72,128]{2,1,0:T(8,128)(2,1)S(1)} %copy-done.3, pred[64]{0:T(512)(128)(4,1)S(1)} %copy-done.18), kind=kOutput, calls=%fused_computation.56 | convolution fusion | flops 306118656 | bytes 10092608 | tf_op jit(solution)/shard_map/rcf,cfo->rco/dot_general | solution.py:32
  310.9 3.1 fusion.66
  315.5 6.2 %all-to-all-start.5 = ((bf16[4,1,18,6144]{3,2,1,0:T(8,128)(2,1)}), bf16[4,1,18,6144]{3,2,1,0:T(8,128)(2,1)S(1)}, u32[]{:S(2)}, u32[]{:S(2)}) async-start(bf16[4,1,18,6144]{3,2,1,0:T(8,128)(2,1)} %bitcast.48), calls=%async_computation.5 | async-start | bytes 2359296 | tf_op jit(solution)/shard_map/all_to_all | solution.py:97
  322.1 24.8 %all-to-all-done.5 = bf16[4,1,18,6144]{3,2,1,0:T(8,128)(2,1)S(1)} async-done(((bf16[4,1,18,6144]{3,2,1,0:T(8,128)(2,1)}), bf16[4,1,18,6144]{3,2,1,0:T(8,128)(2,1)S(1)}, u32[]{:S(2)}, u32[]{:S(2)}) %all-to-all-start.5) | async-done | bytes 884768 | tf_op jit(solution)/shard_map/all_to_all | solution.py:97
  349.2 2.1 multiply_reduce_fusion
  (177 shorter events, 39.3 us)
Async XLA Ops:
  6.5 3.6 %copy-start.1 = (bf16[2,32,6144]{2,1,0:T(8,128)(2,1)S(1)}, bf16[2,32,6144]{2,1,0:T(8,128)(2,1)}, u32[]{:S(2)}) copy-start(bf16[2,32,6144]{2,1,0:T(8,128)(2,1)} %param.11) | copy-start | bytes 2359300
  6.5 38.1 %all-gather.11.cloned.1.call-start = ((), (), s32[]{:S(2)}) async-start(), calls=%async_computation.7 | async-start | bytes 3145728 | tf_op jit(solution)/shard_map/all_gather | solution.py:59
  6.5 3.9 %copy-start.14 = (f32[1,6144]{1,0:T(1,128)S(1)}, f32[1,6144]{1,0:T(1,128)}, u32[]{:S(2)}) copy-start(f32[1,6144]{1,0:T(1,128)} %param.12) | copy-start | bytes 73732
  7.3 70.4 %all-gather.13.cloned.1.call-start = ((), (), s32[]{:S(2)}) async-start(), calls=%async_computation.8 | async-start | bytes 3145728 | tf_op jit(solution)/shard_map/all_gather | solution.py:60
  8.0 104.3 %all-gather.9.cloned.1.call-start = ((), (), s32[]{:S(2)}) async-start(), calls=%async_computation.6 | async-start | bytes 3145728 | tf_op jit(solution)/shard_map/all_gather | solution.py:58
  13.2 4.8 %copy-start.33 = (u32[32]{0:T(128)S(1)}, u32[32]{0:T(128)}, u32[]{:S(2)}) copy-start(u32[32]{0:T(128)} %constant.115) | copy-start | bytes 388
  13.2 5.9 %copy-start.31 = (s32[1,1,32,1]{2,3,1,0:T(1,128)S(1)}, s32[1,1,32,1]{2,3,1,0:T(1,128)}, u32[]{:S(2)}) copy-start(s32[1,1,32,1]{2,3,1,0:T(1,128)} %param.18) | copy-start | bytes 388
  13.2 6.0 %copy-start.32 = (s32[1,1,32,1]{2,3,1,0:T(1,128)S(1)}, s32[1,1,32,1]{2,3,1,0:T(1,128)}, u32[]{:S(2)}) copy-start(s32[1,1,32,1]{2,3,1,0:T(1,128)} %param.19) | copy-start | bytes 388
  13.2 29.9 %all-to-all-start = ((bf16[4,1,18,6144]{3,2,1,0:T(8,128)(2,1)}), bf16[4,1,18,6144]{3,2,1,0:T(8,128)(2,1)S(1)}, u32[]{:S(2)}, u32[]{:S(2)}) async-start(bf16[4,1,18,6144]{3,2,1,0:T(8,128)(2,1)} %select_bitcast_fusion.2), calls=%async_computation | async-start | bytes 2359296 | tf_op jit(solution)/shard_map/all_to_all | solution.py:88
  23.1 95.1 %copy-start.21 = (s32[64]{0:T(128)}, s32[64]{0:T(128)S(1)}, u32[]{:S(2)}) copy-start(s32[64]{0:T(128)S(1)} %get-tuple-element.7) | copy-start | bytes 772
  23.1 20.7 %copy-start.16 = (s32[1024]{0:T(1024)}, s32[1024]{0:T(1024)S(1)}, u32[]{:S(2)}) copy-start(s32[1024]{0:T(1024)S(1)} %pad_clamp_fusion.5) | copy-start | bytes 12292
  23.1 89.3 %copy-start.17 = (pred[64]{0:T(512)(128)(4,1)}, pred[64]{0:T(512)(128)(4,1)S(1)}, u32[]{:S(2)}) copy-start(pred[64]{0:T(512)(128)(4,1)S(1)} %compare_and_fusion) | copy-start | bytes 196
  121.3 6.2 %copy-start.20 = (f32[1,2,32,2]{2,3,1,0:T(2,128)S(1)}, f32[1,2,32,2]{2,3,1,0:T(2,128)}, u32[]{:S(2)}) copy-start(f32[1,2,32,2]{2,3,1,0:T(2,128)} %param.14) | copy-start | bytes 1540
  122.8 29.7 %all-to-all-start.1 = ((bf16[4,1,18,6144]{3,2,1,0:T(8,128)(2,1)}), bf16[4,1,18,6144]{3,2,1,0:T(8,128)(2,1)S(1)}, u32[]{:S(2)}, u32[]{:S(2)}) async-start(bf16[4,1,18,6144]{3,2,1,0:T(8,128)(2,1)} %bitcast.22), calls=%async_computation.1 | async-start | bytes 2359296 | tf_op jit(solution)/shard_map/all_to_all | solution.py:97
  156.8 4.3 %copy-start.15 = (f32[1,6144]{1,0:T(1,128)S(1)}, f32[1,6144]{1,0:T(1,128)}, u32[]{:S(2)}) copy-start(f32[1,6144]{1,0:T(1,128)} %param.12) | copy-start | bytes 73732
  156.9 4.2 %copy-start.9 = (bf16[32,6144]{1,0:T(8,128)(2,1)}, bf16[32,6144]{1,0:T(8,128)(2,1)S(1)}, u32[]{:S(2)}) copy-start(bf16[32,6144]{1,0:T(8,128)(2,1)S(1)} %fusion.98) | copy-start | bytes 1179652
  156.9 3.9 %collective-permute-start = (bf16[32,6144]{1,0:T(8,128)(2,1)S(1)}, bf16[32,6144]{1,0:T(8,128)(2,1)S(1)}, u32[]{:S(2)}, u32[]{:S(2)}) collective-permute-start(bf16[32,6144]{1,0:T(8,128)(2,1)S(1)} %fusion.98), channel_id=1, source_target_pairs={{0,1},{2,3},{4,5},{6,7},{8,9},{10,11},{12,13},{14,15},{16,17},{18,... | collective-permute-start | bytes 1179656 | tf_op jit(solution)/shard_map/ppermute | solution.py:12
  199.6 3.6 %copy-start.4 = (bf16[64,72,128]{2,1,0:T(8,128)(2,1)S(1)}, bf16[64,72,128]{2,1,0:T(8,128)(2,1)}, u32[]{:S(2)}) copy-start(bf16[64,72,128]{2,1,0:T(8,128)(2,1)} %gather_fusion.7) | copy-start | bytes 3538948
  203.3 5.8 %copy-start.22 = (s32[64]{0:T(128)S(1)}, s32[64]{0:T(128)}, u32[]{:S(2)}) copy-start(s32[64]{0:T(128)} %copy-done.21) | copy-start | bytes 772
  212.2 8.6 %copy-start.27 = (s32[1,1,32,2]{2,3,1,0:T(2,128)S(1)}, s32[1,1,32,2]{2,3,1,0:T(2,128)}, u32[]{:S(2)}) copy-start(s32[1,1,32,2]{2,3,1,0:T(2,128)} %get-tuple-element.25) | copy-start | bytes 772
  212.2 8.8 %copy-start.24 = (f32[32,2]{0,1:T(2,128)S(1)}, f32[32,2]{0,1:T(2,128)}, u32[]{:S(2)}) copy-start(f32[32,2]{0,1:T(2,128)} %get-tuple-element.22) | copy-start | bytes 772
  212.2 8.9 %copy-start.26 = (s32[1,1,32,2]{2,3,1,0:T(2,128)S(1)}, s32[1,1,32,2]{2,3,1,0:T(2,128)}, u32[]{:S(2)}) copy-start(s32[1,1,32,2]{2,3,1,0:T(2,128)} %get-tuple-element.11) | copy-start | bytes 772
  213.7 8.2 %copy-start.29 = (s32[64]{0:T(128)S(1)}, s32[64]{0:T(128)}, u32[]{:S(2)}) copy-start(s32[64]{0:T(128)} %copy-done.28) | copy-start | bytes 772
  213.7 32.2 %all-to-all-start.3 = ((bf16[4,1,18,6144]{3,2,1,0:T(8,128)(2,1)}), bf16[4,1,18,6144]{3,2,1,0:T(8,128)(2,1)}, u32[]{:S(2)}, u32[]{:S(2)}) async-start(bf16[4,1,18,6144]{3,2,1,0:T(8,128)(2,1)} %bitcast.35), calls=%async_computation.3 | async-start | bytes 2359296 | tf_op jit(solution)/shard_map/all_to_all | solution.py:97
  252.4 3.6 %copy-start.10 = (bf16[32,6144]{1,0:T(8,128)(2,1)S(1)}, bf16[32,6144]{1,0:T(8,128)(2,1)}, u32[]{:S(2)}) copy-start(bf16[32,6144]{1,0:T(8,128)(2,1)} %copy-done.9) | copy-start | bytes 1179652
  256.0 4.8 %copy-start.2 = (bf16[2,32,6144]{2,1,0:T(8,128)(2,1)S(1)}, bf16[2,32,6144]{2,1,0:T(8,128)(2,1)}, u32[]{:S(2)}) copy-start(bf16[2,32,6144]{2,1,0:T(8,128)(2,1)} %param.11) | copy-start | bytes 2359300
  256.9 4.2 %copy-start.12 = (bf16[32,6144]{1,0:T(8,128)(2,1)}, bf16[32,6144]{1,0:T(8,128)(2,1)S(1)}, u32[]{:S(2)}) copy-start(bf16[32,6144]{1,0:T(8,128)(2,1)S(1)} %get-tuple-element.9) | copy-start | bytes 1179652
  256.9 3.9 %collective-permute-start.1 = (bf16[32,6144]{1,0:T(8,128)(2,1)S(1)}, bf16[32,6144]{1,0:T(8,128)(2,1)S(1)}, u32[]{:S(2)}, u32[]{:S(2)}) collective-permute-start(bf16[32,6144]{1,0:T(8,128)(2,1)S(1)} %get-tuple-element.9), channel_id=1, source_target_pairs={{0,1},{2,3},{4,5},{6,7},{8,9},{10,11},{12,13},{14,15},{16,17},{18,... | collective-permute-start | bytes 1179656 | tf_op jit(solution)/shard_map/ppermute | solution.py:12
  301.4 3.6 %copy-start.3 = (bf16[64,72,128]{2,1,0:T(8,128)(2,1)S(1)}, bf16[64,72,128]{2,1,0:T(8,128)(2,1)}, u32[]{:S(2)}) copy-start(bf16[64,72,128]{2,1,0:T(8,128)(2,1)} %gather_fusion.8) | copy-start | bytes 3538948
  314.0 7.7 %copy-start.25 = (s32[1,1,32,2]{2,3,1,0:T(2,128)S(1)}, s32[1,1,32,2]{2,3,1,0:T(2,128)}, u32[]{:S(2)}) copy-start(s32[1,1,32,2]{2,3,1,0:T(2,128)} %get-tuple-element.10) | copy-start | bytes 772
  314.0 7.9 %copy-start.23 = (f32[32,2]{0,1:T(2,128)S(1)}, f32[32,2]{0,1:T(2,128)}, u32[]{:S(2)}) copy-start(f32[32,2]{0,1:T(2,128)} %get-tuple-element.20) | copy-start | bytes 772
  315.5 31.3 %all-to-all-start.5 = ((bf16[4,1,18,6144]{3,2,1,0:T(8,128)(2,1)}), bf16[4,1,18,6144]{3,2,1,0:T(8,128)(2,1)S(1)}, u32[]{:S(2)}, u32[]{:S(2)}) async-start(bf16[4,1,18,6144]{3,2,1,0:T(8,128)(2,1)} %bitcast.48), calls=%async_computation.5 | async-start | bytes 2359296 | tf_op jit(solution)/shard_map/all_to_all | solution.py:97
  (13 other events, 26.4 us)
Sparse Core Ops, SparseCore 0:
  8.9 34.0 all-gather.10
  44.6 33.0 all-gather.12
  79.2 33.0 all-gather.8
where the time goes:
time: 365 us; the launch traced here: 359 us
  waiting for transfers between devices  162 us (44%)
  blocking collectives  65.9 us (18%)
  local copies, waits for them, and re-layouts  38.1 us (10%)
  matrix products  37.9 us (10%)
  starting transfers between devices  25.3 us (7%)
  other arithmetic  14.8 us (4%)
  between operations  14.4 us (4%)
    all_to_all x3, waiting for transfers between devices, body(): lax.all_to_all(jnp.stack(outputs, 1), 'expert', split_axis=0, concat_axis...  71.6 us
    all_to_all x2, blocking collectives, body(): lax.all_to_all(outgoing, 'expert', split_axis=0, concat_axis=0, tiled=True)  62.2 us
    all_gather x1, waiting for transfers between devices, body(): lax.all_gather(local_blocks[0], 'shard', axis=1, tiled=True)  34.7 us
    all_gather x1, waiting for transfers between devices, body(): lax.all_gather(local_blocks[2], 'shard', axis=1, tiled=True)  29.2 us
    all_to_all x1, waiting for transfers between devices, body(): lax.all_to_all(outgoing, 'expert', split_axis=0, concat_axis=0, tiled=True)  20 us
    all_to_all x3, starting transfers between devices, body(): lax.all_to_all(jnp.stack(outputs, 1), 'expert', split_axis=0, concat_axis...  17.9 us
    dot_general x3, matrix products, hidden_part(): jnp.einsum('rcf,cfo->rco', hidden, down_w[:, 0], preferred_element_type=j...  17.5 us
    dot_general x3, matrix products, hidden_part(): jnp.einsum('rckd,ckdf->rcf', picked, up_w, preferred_element_type=jnp.flo...  11.1 us
  transfers between devices with their start and end apart: 9, of which 8 were waited for; matrix products, arithmetic and copies ran while one was open for 4% of the time, Pallas kernels for 0%

commit v1 on v0

v1 whole, which is shorter than its diff:
```python
import functools

import jax
import jax.numpy as jnp
from jax import lax
from jax.experimental import pallas as pl
from jax.experimental.pallas import tpu as pltpu
from jax.sharding import PartitionSpec as P

TOP = 2
EPS = 1e-05
BF16 = jnp.bfloat16
F32 = jnp.float32


def layer_kernel(
    dims,
    tokens, gain, disp, comb, gate_hbm, up_hbm, down_hbm, meta_hbm,
    out,
    held, normed, wide, send, recv, parts, ret_send, ret_recv, weights, meta_v, meta_s,
    tok_sem, hand_sem, own_sem, meta_own_sem, meta_send_sem, meta_recv_sem, meta_copy_sem,
    wx_send, wx_recv, wy_send, wy_recv, disp_send, disp_recv, disp_self,
    back_send, back_recv, back_self, go_sem,
):
    micro, rows, blocks, blk, cap, experts, shards, groups, sections, n_blk = dims
    slots = experts * cap
    me_g, me_s = lax.axis_index("groups"), lax.axis_index("shard")
    me_e, me_l = lax.axis_index("expert"), lax.axis_index("section")
    sizes = {"groups": groups, "shard": shards, "expert": experts, "section": sections}
    place = {"groups": me_g, "shard": me_s, "expert": me_e, "section": me_l}
    half = n_blk // groups
    cuts = 2 if half % 2 == 0 else 1
    step = half // cuts
    sources = (gate_hbm, up_hbm, down_hbm)

    def remote(src, dst, ssem, rsem, axis, index):
        return pltpu.make_async_remote_copy(
            src_ref=src, dst_ref=dst, send_sem=ssem, recv_sem=rsem,
            device_id={axis: index}, device_id_type=pl.DeviceIdType.MESH,
        )

    def peer(axis, by):
        return lax.rem(place[axis] + by, sizes[axis])

    own = [
        pltpu.make_async_copy(sources[a], weights.at[a, me_s], own_sem.at[a]) for a in range(3)
    ]
    for copy in own:
        copy.start()
    meta_own = pltpu.make_async_copy(meta_hbm, meta_v.at[me_s], meta_own_sem)
    meta_own.start()

    barrier = pltpu.get_barrier_semaphore()
    for axis in ("groups", "shard", "expert", "section"):
        for by in range(1, sizes[axis]):
            pl.semaphore_signal(
                barrier, inc=1, device_id={axis: peer(axis, by)},
                device_id_type=pl.DeviceIdType.MESH,
            )
    pl.semaphore_wait(barrier, sum(n - 1 for n in sizes.values()))

    def token_copy(m):
        return pltpu.make_async_copy(tokens.at[m], held.at[m], tok_sem.at[m])

    def hand_copy(m):
        return remote(
            out.at[m], held.at[m], hand_sem.at[0, m], hand_sem.at[1, m], "section",
            peer("section", 1),
        )

    def part(group, a, k, shard):
        return weights.at[a, shard, pl.ds(group * half + k * step, step)]

    def over_shard(a, k, by):
        i = k * 3 + a
        src = sources[a].at[pl.ds(me_g * half + k * step, step)]
        return remote(
            src, part(me_g, a, k, me_s), wx_send.at[i, by], wx_recv.at[i, by], "shard",
            peer("shard", by),
        )

    def over_groups(a, k, by, hop):
        i = k * 3 + a
        spot = part(me_g, a, k, peer("shard", shards - by))
        return remote(
            spot, spot, wy_send.at[i, by, hop], wy_recv.at[i, by, hop], "groups",
            peer("groups", hop),
        )

    def meta_over_shard(by):
        return remote(
            meta_hbm, meta_v.at[me_s], meta_send_sem.at[by], meta_recv_sem.at[by], "shard",
            peer("shard", by),
        )

    order = [(a, k, by) for k in range(cuts) for a in range(3) for by in range(1, shards)]

    def start_weights():
        for by in range(1, shards):
            meta_over_shard(by).start()
        for a, k, by in order:
            over_shard(a, k, by).start()

    def relay_weights():
        for a, k, by in order:
            over_shard(a, k, by).wait_recv()
            for hop in range(1, groups):
                over_groups(a, k, by, hop).start()

    def finish_weights():
        for by in range(1, shards):
            meta_over_shard(by).wait()
        for a, k, by in order:
            over_shard(a, k, by).wait_send()
            for hop in range(1, groups):
                over_groups(a, k, by, hop).wait()

    def chunk_out(m, by):
        return remote(
            send.at[m, peer("expert", by)], recv.at[m, me_e], disp_send.at[m, by],
            disp_recv.at[m, by], "expert", peer("expert", by),
        )

    def chunk_self(m):
        return pltpu.make_async_copy(send.at[m, me_e], recv.at[m, me_e], disp_self.at[m])

    def chunk_back(m, by):
        return remote(
            ret_send.at[m, peer("expert", by)], ret_recv.at[m, me_e], back_send.at[m, by],
            back_recv.at[m, by], "expert", peer("expert", by),
        )

    def back_own(m):
        return pltpu.make_async_copy(ret_send.at[m, me_e], ret_recv.at[m, me_e], back_self.at[m])

    far_first = sorted(range(1, experts), key=lambda by: abs(by - experts // 2))

    def lanes(r):
        return pl.ds(pl.multiple_of(r * blk, blk), blk)

    def strided(r):
        return pl.ds(r, slots, stride=blocks)

    def dispatch(m):
        values = held[m].astype(F32)
        scale = lax.rsqrt(jnp.mean(values * values, axis=-1, keepdims=True) + EPS)
        normed[...] = (values * scale * gain[...]).astype(BF16)

        @pl.loop(0, blocks, unroll=8)
        def _(r):
            wide[strided(r), :] = jnp.dot(
                disp[m], normed[:, lanes(r)], preferred_element_type=F32
            )

        for e in range(experts):
            send[m, e] = wide[pl.ds(e * cap * blocks, cap * blocks), :].astype(BF16)
        for by in far_first:
            chunk_out(m, by).start()
        chunk_self(m).start()

    def shard_part(s):
        several = min(8, n_blk)

        @pl.loop(0, n_blk // several)
        def _(q):
            products = []
            for u in range(several):
                c = q * several + u
                x = wide[strided(meta_s[s, 0, c]), :].astype(BF16)
                gate = jnp.dot(x, weights[0, s, c], preferred_element_type=F32)
                up = jnp.dot(x, weights[1, s, c], preferred_element_type=F32)
                hidden = (gate / (1.0 + jnp.exp(-gate)) * up).astype(BF16)
                products.append(jnp.dot(hidden, weights[2, s, c], preferred_element_type=F32))
            for u in range(several):
                c = q * several + u
                parts[s, c] = products[u] + parts[s, meta_s[s, 0, n_blk + c]]

    def expert_part(m, first):
        for by in range(1, experts):
            chunk_out(m, by).wait()
        chunk_self(m).wait()
        for e in range(experts):
            wide[pl.ds(e * cap * blocks, cap * blocks), :] = recv[m, e].astype(F32)
        if first:
            for copy in own:
                copy.wait()
            finish_weights()
            meta_own.wait()
            load = pltpu.make_async_copy(meta_v, meta_s, meta_copy_sem)
            load.start()
            load.wait()

        @pl.loop(0, shards)
        def _(s):
            shard_part(s)

        @pl.loop(0, blocks, unroll=4)
        def _(j):
            total = parts[0, meta_s[0, 0, 2 * n_blk + j]]
            for s in range(1, shards):
                total = total + parts[s, meta_s[s, 0, 2 * n_blk + j]]
            wide[strided(j), :] = total

        for e in range(experts):
            ret_send[m, e] = wide[pl.ds(e * cap * blocks, cap * blocks), :].astype(BF16)
        for by in far_first:
            chunk_back(m, by).start()
        back_own(m).start()

    def combine(m):
        for by in range(1, experts):
            chunk_back(m, by).wait()
        back_own(m).wait()
        for e in range(experts):
            wide[pl.ds(e * cap * blocks, cap * blocks), :] = ret_recv[m, e].astype(F32)

        @pl.loop(0, blocks, unroll=8)
        def _(r):
            mixed = jnp.dot(
                comb[m], wide[strided(r), :], preferred_element_type=F32,
                precision=lax.Precision.HIGHEST,
            )
            out[m, :, lanes(r)] = (held[m, :, lanes(r)].astype(F32) + mixed).astype(BF16)

    for s in range(shards):
        parts[s, n_blk] = jnp.zeros_like(parts[s, n_blk])

    @pl.when(me_l == 0)
    def _():
        for m in range(micro):
            token_copy(m).start()
        start_weights()
        for m in range(micro):
            token_copy(m).wait()
            dispatch(m)
        relay_weights()

    @pl.when(me_l > 0)
    def _():
        pl.semaphore_wait(go_sem, 1)
        start_weights()
        relay_weights()

    @pl.when(me_l < sections - 1)
    def _():
        pl.semaphore_signal(
            go_sem, inc=1, device_id={"section": peer("section", 1)},
            device_id_type=pl.DeviceIdType.MESH,
        )

    @pl.when(me_l > 0)
    def _():
        for m in range(micro):
            hand_copy(m).wait_recv()
            dispatch(m)

    for m in range(micro):
        expert_part(m, m == 0)
    for m in range(micro):
        combine(m)

        @pl.when(me_l < sections - 1)
        def _():
            hand_copy(m).start()

    @pl.when(me_l < sections - 1)
    def _():
        for m in range(micro):
            hand_copy(m).wait_send()


def body(
    sizes,
    tokens,
    norm_gain,
    route_ids,
    route_weights,
    gate_blocks,
    up_blocks,
    down_blocks,
    gate_rows,
    down_cols,
):
    groups, shards, experts, sections = sizes
    micro, rows, width = tokens.shape
    n_blk, blk = gate_blocks.shape[2], gate_blocks.shape[-1]
    blocks = width // blk
    cap = min(rows, max(rows * 9 // 16, rows * TOP // experts + 2))
    slots = experts * cap

    ids, mix = route_ids[0], route_weights[0]
    named = ids[..., None] == jnp.arange(experts, dtype=jnp.int32)
    hit = jnp.any(named, axis=2)
    amount = jnp.sum(jnp.where(named, mix[..., None], 0.0), axis=2)
    earlier = jnp.arange(rows)[None, :] < jnp.arange(rows)[:, None]
    ahead = jnp.sum(
        jnp.where(earlier[None, :, :, None] & hit[:, None, :, :], 1, 0).astype(jnp.int32), axis=2
    )
    fits = hit[..., None] & (ahead[..., None] == jnp.arange(cap, dtype=jnp.int32))
    fits = fits.reshape(micro, rows, slots)
    comb = jnp.where(fits, jnp.repeat(amount, cap, axis=2), 0.0)
    disp = jnp.swapaxes(fits, 1, 2).astype(BF16)

    cols = down_cols[0, 0, :, 0]
    number = jnp.arange(n_blk, dtype=jnp.int32)
    same = (cols[:, None] == cols[None, :]) & (number[None, :] < number[:, None])
    before = jnp.max(jnp.where(same, number[None, :], -1), axis=1)
    before = jnp.where(before < 0, n_blk, before)
    here = cols[None, :] == jnp.arange(blocks, dtype=jnp.int32)[:, None]
    last = jnp.max(jnp.where(here, number[None, :], -1), axis=1)
    last = jnp.where(last < 0, n_blk, last)
    meta = jnp.concatenate([gate_rows[0, 0, :, 0], before, last])
    meta_width = -(-meta.shape[0] // 128) * 128
    meta = jnp.pad(meta, (0, meta_width - meta.shape[0]))[None]

    half = n_blk // groups
    pieces = 3 * (2 if half % 2 == 0 else 1)
    dims = (micro, rows, blocks, blk, cap, experts, shards, groups, sections, n_blk)
    dma = pltpu.SemaphoreType.DMA
    chunk = (micro, experts, cap * blocks, blk)
    vmem, anywhere = pl.BlockSpec(memory_space=pltpu.VMEM), pl.BlockSpec(memory_space=pl.ANY)
    out = pl.pallas_call(
        functools.partial(layer_kernel, dims),
        out_shape=jax.ShapeDtypeStruct((micro, rows, width), BF16),
        in_specs=[anywhere, vmem, vmem, vmem, anywhere, anywhere, anywhere, anywhere],
        out_specs=vmem,
        scratch_shapes=[
            pltpu.VMEM((micro, rows, width), BF16),
            pltpu.VMEM((rows, width), BF16),
            pltpu.VMEM((slots * blocks, blk), F32),
            pltpu.VMEM(chunk, BF16),
            pltpu.VMEM(chunk, BF16),
            pltpu.VMEM((shards, n_blk + 1, slots, blk), F32),
            pltpu.VMEM(chunk, BF16),
            pltpu.VMEM(chunk, BF16),
            pltpu.VMEM((3, shards, n_blk, blk, blk), BF16),
            pltpu.VMEM((shards, 1, meta_width), jnp.int32),
            pltpu.SMEM((shards, 1, meta_width), jnp.int32),
            dma((micro,)),
            dma((2, micro)),
            dma((3,)),
            dma,
            dma((shards,)),
            dma((shards,)),
            dma,
            dma((pieces, shards)),
            dma((pieces, shards)),
            dma((pieces, shards, groups)),
            dma((pieces, shards, groups)),
            dma((micro, experts)),
            dma((micro, experts)),
            dma((micro,)),
            dma((micro, experts)),
            dma((micro, experts)),
            dma((micro,)),
            pltpu.SemaphoreType.REGULAR,
        ],
        compiler_params=pltpu.CompilerParams(
            collective_id=0, has_side_effects=True, vmem_limit_bytes=56 * 1024 * 1024
        ),
    )(
        tokens, norm_gain, disp, comb,
        gate_blocks.reshape(n_blk, blk, blk), up_blocks.reshape(n_blk, blk, blk),
        down_blocks.reshape(n_blk, blk, blk), meta,
    )
    return out[None]


def solution(mesh):
    sizes = tuple(mesh.shape[name] for name in ("groups", "shard", "expert", "section"))
    in_specs = (
        P(None, ("groups", "shard", "expert"), None),
        P("section", None),
        P("section", None, ("groups", "shard", "expert"), None),
        P("section", None, ("groups", "shard", "expert"), None),
        P("section", "expert", "shard", None, None, None),
        P("section", "expert", "shard", None, None, None),
        P("section", "expert", "shard", None, None, None),
        P("section", "expert", "shard", None),
        P("section", "expert", "shard", None),
    )
    out_specs = P("section", None, ("groups", "shard", "expert"), None)
    return jax.shard_map(
        functools.partial(body, sizes), mesh=mesh, in_specs=in_specs, out_specs=out_specs,
        check_vma=False,
    )
```

time: 365 us -> 106 us (0.29); the launches traced: 359 us -> 105 us
  waiting for transfers between devices: 162 us -> 0 us
  Pallas kernels: 0 us -> 98.1 us
  blocking collectives: 65.9 us -> 0 us
  matrix products: 37.9 us -> 0 us
  local copies, waits for them, and re-layouts: 38.1 us -> 5.91 us
  starting transfers between devices: 25.3 us -> 0 us
  between operations: 14.4 us -> 0.09 us
  other arithmetic: 14.8 us -> 1.24 us
    pallas_call x0 -> x1, Pallas kernels: none -> 98.1 us  [body(): pl.pallas_call(functools.partial(layer_kernel, dims), out_shape=jax.Shape...]
    all_to_all x4 -> x0, waiting for transfers between devices: 91.6 us -> none  [the longest x3 71.6 us: body(): lax.all_to_all(jnp.stack(outputs, 1), 'expert', split_axis=0, concat_axis...]
    all_gather x3 -> x0, waiting for transfers between devices: 63.9 us -> none  [the longest x1 34.7 us: body(): lax.all_gather(local_blocks[0], 'shard', axis=1, tiled=True)]
    all_to_all x2 -> x0, blocking collectives: 62.2 us -> none  [body(): lax.all_to_all(outgoing, 'expert', split_axis=0, concat_axis=0, tiled=True)]
    dot_general x9 -> x0, matrix products: 37.9 us -> none  [the longest x3 17.5 us: hidden_part(): jnp.einsum('rcf,cfo->rco', hidden, down_w[:, 0], preferred_element_type=j...]
    all_to_all x4 -> x0, starting transfers between devices: 22.7 us -> none  [the longest x3 17.9 us: body(): lax.all_to_all(jnp.stack(outputs, 1), 'expert', split_axis=0, concat_axis...]
    gather x12 -> x0, local copies, waits for them, and re-layouts: 14.7 us -> none  [the longest x6 6.2 us: body(): normed[source]]
    reduce_sum x12 -> x2, other arithmetic: 9.23 us -> 0.24 us  [the longest x1 0.22 us: body(): jnp.sum(jnp.where(earlier[None, :, :, None] & hit[:, None, :, :], 1, 0).a...]
  transfers between devices with their start and end apart: 9 -> 0, of which waited for: 8 -> 0; matrix products, arithmetic and copies ran while one was open for 4% -> 0% of each run, Pallas kernels for 0% -> 0%
where the time goes in v1:
time: 106 us; the launch traced here: 105 us
  Pallas kernels  98.1 us (93%)
  local copies, waits for them, and re-layouts  5.91 us (6%)
  other arithmetic  1.24 us (1%)
    pallas_call x1, Pallas kernels, body(): pl.pallas_call(functools.partial(layer_kernel, dims), out_shape=jax.Shape...  98.1 us
    unnamed x9, local copies, waits for them, and re-layouts  4 us

profile of v1, /device:TPU:17, one launch (start us, length us, event | category | flops | bytes accessed | tf_op | source)
XLA Modules:
  0.0 105.3 jit_solution(3439356774429226909)
XLA Ops:
  0.0 0.0 copy-start.3
  0.0 0.7 copy-done.3
  0.7 0.2 select_reduce_fusion.2
  0.8 0.1 select_reduce_fusion.1
  0.9 0.0 copy-start.2
  1.0 0.6 copy-done.2
  1.6 0.0 copy-start
  1.6 0.1 pad_add_fusion
  1.7 0.5 pad_bitcast_fusion.meta_hbm
  2.2 0.1 copy-done
  2.3 0.0 copy-start.1
  2.3 0.1 eq.70
  2.4 0.6 copy-done.1
  3.0 0.2 select_reduce_fusion
  3.2 0.1 copy.18
  3.4 0.1 and.27
  3.5 0.1 and.28
  3.6 0.1 copy.20
  3.7 0.1 copy.22
  3.8 0.6 broadcast_select_fusion
  4.4 0.7 copy.23.disp
  5.2 98.1 %shard_map.91 = bf16[2,32,6144]{2,1,0:T(8,128)(2,1)} custom-call(bf16[2,32,6144]{2,1,0:T(8,128)(2,1)} %tokens.1, f32[1,6144]{1,0:T(1,128)} %gain.1, bf16[2,72,32]{2,1,0:T(8,128)(2,1)} %copy.23.disp, f32[2,32,72]{2,1,0:T(8,128)} %get-tuple-element.5.comb, bf16[32,128,128]{2,1,0:T(8,128)(2,1)} %bitcast.15, bf16[32,128,128]{2,1,0:T(8,128)(2,1)} %bitcast.16, ...), custom_call_target="tpu_custom_call" | custom-call | tf_op jit(solution)/shard_map/pallas_call | solution.py:322
  103.3 2.1 %copy.25 = bf16[1,2,32,6144]{3,2,1,0:T(8,128)(2,1)} copy(bf16[1,2,32,6144]{3,2,1,0:T(8,128)(2,1)} %bitcast.14) | data formatting | bytes 1572864
  (11 shorter events, 0.1 us)
Async XLA Ops:
  0.0 0.7 copy-start.3
  0.9 0.7 copy-start.2
  1.6 0.7 copy-start
  2.3 0.7 copy-start.1

commit v2 on v1

--- a/solution.py
+++ b/solution.py
@@ -1,4 +1,5 @@
 import functools
+import math
 
 import jax
 import jax.numpy as jnp
@@ -15,9 +16,9 @@
 
 def layer_kernel(
     dims,
-    tokens, gain, disp, comb, gate_hbm, up_hbm, down_hbm, meta_hbm,
+    tokens, gain, ids, mix, gate_hbm, up_hbm, down_hbm, rows_in, cols_in,
     out,
-    held, normed, wide, send, recv, parts, ret_send, ret_recv, weights, meta_v, meta_s,
+    held, disp, comb, meta_here, normed, wide, send, recv, parts, ret_send, ret_recv, weights, meta_v, meta_s,
     tok_sem, hand_sem, own_sem, meta_own_sem, meta_send_sem, meta_recv_sem, meta_copy_sem,
     wx_send, wx_recv, wy_send, wy_recv, disp_send, disp_recv, disp_self,
     back_send, back_recv, back_self, go_sem,
@@ -29,7 +30,7 @@
     sizes = {"groups": groups, "shard": shards, "expert": experts, "section": sections}
     place = {"groups": me_g, "shard": me_s, "expert": me_e, "section": me_l}
     half = n_blk // groups
-    cuts = 2 if half % 2 == 0 else 1
+    cuts = math.gcd(half, 4)
     step = half // cuts
     sources = (gate_hbm, up_hbm, down_hbm)
 
@@ -47,8 +48,7 @@
     ]
     for copy in own:
         copy.start()
-    meta_own = pltpu.make_async_copy(meta_hbm, meta_v.at[me_s], meta_own_sem)
-    meta_own.start()
+    meta_own = pltpu.make_async_copy(meta_here, meta_v.at[me_s], meta_own_sem)
 
     barrier = pltpu.get_barrier_semaphore()
     for axis in ("groups", "shard", "expert", "section"):
@@ -57,7 +57,46 @@
                 barrier, inc=1, device_id={axis: peer(axis, by)},
                 device_id_type=pl.DeviceIdType.MESH,
             )
+
+    def arrival(c):
+        group = sum((c >= g * half).astype(jnp.int32) for g in range(1, groups))
+        within = c - group * half
+        k = sum((within >= i * step).astype(jnp.int32) for i in range(1, cuts))
+        return k * (groups - 1) * step + group * step + within
+
+    def iota(shape, axis):
+        return lax.broadcasted_iota(jnp.int32, shape, axis)
+
+    cols = cols_in[...]
+    cols_down = jnp.transpose(jnp.broadcast_to(cols, (n_blk, n_blk)))
+    from_place = arrival(iota((n_blk, n_blk), 0))
+    chained = (cols_down == cols) & (from_place < arrival(iota((n_blk, n_blk), 1)))
+    before = jnp.max(jnp.where(chained, from_place, -1), axis=0, keepdims=True)
+    final = jnp.broadcast_to(cols_down[:, :1], (n_blk, blocks)) == iota((n_blk, blocks), 1)
+    last = jnp.where(final, arrival(iota((n_blk, blocks), 0)), -1)
+    last = jnp.max(last, axis=0, keepdims=True)
+    meta_here[...] = jnp.zeros_like(meta_here)
+    meta_here[0:1, 0:n_blk] = rows_in[...]
+    meta_here[1:2, 0:n_blk] = jnp.where(before < 0, n_blk, before)
+    meta_here[2:3, 0:blocks] = jnp.where(last < 0, n_blk, last)
+
+    slot = iota((slots, rows), 0)
+    expert = sum((slot >= e * cap).astype(jnp.int32) for e in range(1, experts))
+    place_in = (slot - expert * cap).astype(F32)
+    earlier = (iota((rows, rows), 0) < iota((rows, rows), 1)).astype(F32).astype(BF16)
+    for m in range(micro):
+        named = [ids[m, j:j + 1, :] == expert for j in range(TOP)]
+        hit = functools.reduce(jnp.logical_or, named)
+        ahead = jnp.dot(
+            hit.astype(F32).astype(BF16), earlier, preferred_element_type=F32
+        )
+        fits = hit & (ahead == place_in)
+        amount = sum(jnp.where(named[j], mix[m, j:j + 1, :], 0.0) for j in range(TOP))
+        disp[m] = fits.astype(F32).astype(BF16)
+        comb[m] = jnp.transpose(jnp.where(fits, amount, 0.0))
+
     pl.semaphore_wait(barrier, sum(n - 1 for n in sizes.values()))
+    meta_own.start()
 
     def token_copy(m):
         return pltpu.make_async_copy(tokens.at[m], held.at[m], tok_sem.at[m])
@@ -89,7 +128,7 @@
 
     def meta_over_shard(by):
         return remote(
-            meta_hbm, meta_v.at[me_s], meta_send_sem.at[by], meta_recv_sem.at[by], "shard",
+            meta_here, meta_v.at[me_s], meta_send_sem.at[by], meta_recv_sem.at[by], "shard",
             peer("shard", by),
         )
 
@@ -101,19 +140,25 @@
         for a, k, by in order:
             over_shard(a, k, by).start()
 
-    def relay_weights():
+    def relay_weights(first, end):
         for a, k, by in order:
-            over_shard(a, k, by).wait_recv()
-            for hop in range(1, groups):
-                over_groups(a, k, by, hop).start()
-
-    def finish_weights():
-        for by in range(1, shards):
-            meta_over_shard(by).wait()
+            if first <= k < end:
+                over_shard(a, k, by).wait_recv()
+                for hop in range(1, groups):
+                    over_groups(a, k, by, hop).start()
+
+    def finish_relay(at):
         for a, k, by in order:
-            over_shard(a, k, by).wait_send()
-            for hop in range(1, groups):
-                over_groups(a, k, by, hop).wait()
+            if k == at:
+                for hop in range(1, groups):
+                    over_groups(a, k, by, hop).wait()
+
+    early = cuts
+
+    def relay_in_time(first, end):
+        @pl.when(me_l == 0)
+        def _():
+            relay_weights(first, end)
 
     def chunk_out(m, by):
         return remote(
@@ -158,22 +203,20 @@
             chunk_out(m, by).start()
         chunk_self(m).start()
 
-    def shard_part(s):
-        several = min(8, n_blk)
-
-        @pl.loop(0, n_blk // several)
-        def _(q):
-            products = []
-            for u in range(several):
-                c = q * several + u
+    def segment(s, k):
+        products = []
+        for group in range(groups):
+            for u in range(step):
+                c = group * half + k * step + u
+                at = (k * groups + group) * step + u
                 x = wide[strided(meta_s[s, 0, c]), :].astype(BF16)
                 gate = jnp.dot(x, weights[0, s, c], preferred_element_type=F32)
                 up = jnp.dot(x, weights[1, s, c], preferred_element_type=F32)
                 hidden = (gate / (1.0 + jnp.exp(-gate)) * up).astype(BF16)
-                products.append(jnp.dot(hidden, weights[2, s, c], preferred_element_type=F32))
-            for u in range(several):
-                c = q * several + u
-                parts[s, c] = products[u] + parts[s, meta_s[s, 0, n_blk + c]]
+                product = jnp.dot(hidden, weights[2, s, c], preferred_element_type=F32)
+                products.append((at, c, product))
+        for at, c, product in products:
+            parts[s, at] = product + parts[s, meta_s[s, 1, c]]
 
     def expert_part(m, first):
         for by in range(1, experts):
@@ -184,21 +227,49 @@
         if first:
             for copy in own:
                 copy.wait()
-            finish_weights()
+            for by in range(1, shards):
+                meta_over_shard(by).wait()
             meta_own.wait()
             load = pltpu.make_async_copy(meta_v, meta_s, meta_copy_sem)
             load.start()
             load.wait()
 
-        @pl.loop(0, shards)
-        def _(s):
-            shard_part(s)
+            @pl.loop(0, cuts)
+            def _(k):
+                segment(me_s, k)
+
+            for k in range(cuts):
+                if k == 0:
+                    relay_in_time(early, min(early + 1, cuts))
+                elif early + k < cuts:
+                    relay_in_time(early + k, early + k + 1)
+                finish_relay(k)
+
+                @pl.loop(1, shards)
+                def _(by):
+                    segment(peer("shard", shards - by), k)
+
+                if k == max(0, cuts - early - 1):
+                    @pl.when((me_l == 0) & (me_l < sections - 1))
+                    def _():
+                        pl.semaphore_signal(
+                            go_sem, inc=1, device_id={"section": peer("section", 1)},
+                            device_id_type=pl.DeviceIdType.MESH,
+                        )
+            for a, k, by in order:
+                over_shard(a, k, by).wait_send()
+        else:
+            @pl.loop(0, shards)
+            def _(s):
+                @pl.loop(0, cuts)
+                def _(k):
+                    segment(s, k)
 
         @pl.loop(0, blocks, unroll=4)
         def _(j):
-            total = parts[0, meta_s[0, 0, 2 * n_blk + j]]
+            total = parts[0, meta_s[0, 2, j]]
             for s in range(1, shards):
-                total = total + parts[s, meta_s[s, 0, 2 * n_blk + j]]
+                total = total + parts[s, meta_s[s, 2, j]]
             wide[strided(j), :] = total
 
         for e in range(experts):
@@ -233,15 +304,15 @@
         for m in range(micro):
             token_copy(m).wait()
             dispatch(m)
-        relay_weights()
+        relay_weights(0, early)
 
     @pl.when(me_l > 0)
     def _():
         pl.semaphore_wait(go_sem, 1)
         start_weights()
-        relay_weights()
-
-    @pl.when(me_l < sections - 1)
+        relay_weights(0, cuts)
+
+    @pl.when((me_l > 0) & (me_l < sections - 1))
     def _():
         pl.semaphore_signal(
             go_sem, inc=1, device_id={"section": peer("section", 1)},
@@ -288,33 +359,9 @@
     cap = min(rows, max(rows * 9 // 16, rows * TOP // experts + 2))
     slots = experts * cap
 
-    ids, mix = route_ids[0], route_weights[0]
-    named = ids[..., None] == jnp.arange(experts, dtype=jnp.int32)
-    hit = jnp.any(named, axis=2)
-    amount = jnp.sum(jnp.where(named, mix[..., None], 0.0), axis=2)
-    earlier = jnp.arange(rows)[None, :] < jnp.arange(rows)[:, None]
-    ahead = jnp.sum(
-        jnp.where(earlier[None, :, :, None] & hit[:, None, :, :], 1, 0).astype(jnp.int32), axis=2
-    )
-    fits = hit[..., None] & (ahead[..., None] == jnp.arange(cap, dtype=jnp.int32))
-    fits = fits.reshape(micro, rows, slots)
-    comb = jnp.where(fits, jnp.repeat(amount, cap, axis=2), 0.0)
-    disp = jnp.swapaxes(fits, 1, 2).astype(BF16)
-
-    cols = down_cols[0, 0, :, 0]
-    number = jnp.arange(n_blk, dtype=jnp.int32)
-    same = (cols[:, None] == cols[None, :]) & (number[None, :] < number[:, None])
-    before = jnp.max(jnp.where(same, number[None, :], -1), axis=1)
-    before = jnp.where(before < 0, n_blk, before)
-    here = cols[None, :] == jnp.arange(blocks, dtype=jnp.int32)[:, None]
-    last = jnp.max(jnp.where(here, number[None, :], -1), axis=1)
-    last = jnp.where(last < 0, n_blk, last)
-    meta = jnp.concatenate([gate_rows[0, 0, :, 0], before, last])
-    meta_width = -(-meta.shape[0] // 128) * 128
-    meta = jnp.pad(meta, (0, meta_width - meta.shape[0]))[None]
-
-    half = n_blk // groups
-    pieces = 3 * (2 if half % 2 == 0 else 1)
+    cuts = math.gcd(n_blk // groups, 4)
+    meta_width = -(-max(n_blk, blocks) // 128) * 128
+    pieces = 3 * cuts
     dims = (micro, rows, blocks, blk, cap, experts, shards, groups, sections, n_blk)
     dma = pltpu.SemaphoreType.DMA
     chunk = (micro, experts, cap * blocks, blk)
@@ -322,10 +369,13 @@
     out = pl.pallas_call(
         functools.partial(layer_kernel, dims),
         out_shape=jax.ShapeDtypeStruct((micro, rows, width), BF16),
-        in_specs=[anywhere, vmem, vmem, vmem, anywhere, anywhere, anywhere, anywhere],
+        in_specs=[anywhere] + [vmem] * 3 + [anywhere] * 3 + [vmem] * 2,
         out_specs=vmem,
         scratch_shapes=[
             pltpu.VMEM((micro, rows, width), BF16),
+            pltpu.VMEM((micro, slots, rows), BF16),
+            pltpu.VMEM((micro, rows, slots), F32),
+            pltpu.VMEM((8, meta_width), jnp.int32),
             pltpu.VMEM((rows, width), BF16),
             pltpu.VMEM((slots * blocks, blk), F32),
             pltpu.VMEM(chunk, BF16),
@@ -334,8 +384,8 @@
             pltpu.VMEM(chunk, BF16),
             pltpu.VMEM(chunk, BF16),
             pltpu.VMEM((3, shards, n_blk, blk, blk), BF16),
-            pltpu.VMEM((shards, 1, meta_width), jnp.int32),
-            pltpu.SMEM((shards, 1, meta_width), jnp.int32),
+            pltpu.VMEM((shards, 8, meta_width), jnp.int32),
+            pltpu.SMEM((shards, 8, meta_width), jnp.int32),
             dma((micro,)),
             dma((2, micro)),
             dma((3,)),
@@ -359,9 +409,10 @@
             collective_id=0, has_side_effects=True, vmem_limit_bytes=56 * 1024 * 1024
         ),
     )(
-        tokens, norm_gain, disp, comb,
+        tokens, norm_gain, jnp.swapaxes(route_ids[0], 1, 2), jnp.swapaxes(route_weights[0], 1, 2),
         gate_blocks.reshape(n_blk, blk, blk), up_blocks.reshape(n_blk, blk, blk),
-        down_blocks.reshape(n_blk, blk, blk), meta,
+        down_blocks.reshape(n_blk, blk, blk), gate_rows.reshape(1, n_blk),
+        down_cols.reshape(1, n_blk),
     )
     return out[None]
 

time: 106 us -> 97.1 us (0.916)
  local copies, waits for them, and re-layouts: 5.91 us -> 2.06 us
  Pallas kernels: 98.1 us -> 94.8 us
  other arithmetic: 1.24 us -> 0 us
    pallas_call x1, Pallas kernels: 98.1 us -> 94.8 us  [body(): pl.pallas_call(functools.partial(layer_kernel, dims), out_shape=jax.Shape...]
    unnamed x9 -> x1, local copies, waits for them, and re-layouts: 4 us -> 2.06 us
where the time goes in v2:
time: 97.1 us; the launch traced here: 96.8 us
  Pallas kernels  94.8 us (98%)
  local copies, waits for them, and re-layouts  2.06 us (2%)
    pallas_call x1, Pallas kernels, body(): pl.pallas_call(functools.partial(layer_kernel, dims), out_shape=jax.Shape...  94.8 us
    unnamed x1, local copies, waits for them, and re-layouts  2.06 us

profile of v2, /device:TPU:17, one launch (start us, length us, event | category | flops | bytes accessed | tf_op | source)
XLA Modules:
  0.0 96.8 jit_solution(4623541177737656295)
XLA Ops:
  0.0 94.8 %shard_map.91 = bf16[2,32,6144]{2,1,0:T(8,128)(2,1)} custom-call(bf16[2,32,6144]{2,1,0:T(8,128)(2,1)} %tokens.1, f32[1,6144]{1,0:T(1,128)} %gain.1, s32[2,2,32]{2,1,0:T(2,128)} %bitcast.16, f32[2,2,32]{2,1,0:T(2,128)} %bitcast.17, bf16[32,128,128]{2,1,0:T(8,128)(2,1)} %bitcast.13, bf16[32,128,128]{2,1,0:T(8,128)(2,1)} %bitcast.14, ...), custom_call_target="tpu_custom_call" | custom-call | tf_op jit(solution)/shard_map/pallas_call | solution.py:369
  94.8 2.1 %copy.11 = bf16[1,2,32,6144]{3,2,1,0:T(8,128)(2,1)} copy(bf16[1,2,32,6144]{3,2,1,0:T(8,128)(2,1)} %bitcast.12) | data formatting | bytes 1572864

commit v3 on v2

--- a/solution.py
+++ b/solution.py
@@ -48,6 +48,15 @@
     ]
     for copy in own:
         copy.start()
+
+    def token_copy(m):
+        return pltpu.make_async_copy(tokens.at[m], held.at[m], tok_sem.at[m])
+
+    @pl.when(me_l == 0)
+    def _():
+        for m in range(micro):
+            token_copy(m).start()
+
     meta_own = pltpu.make_async_copy(meta_here, meta_v.at[me_s], meta_own_sem)
 
     barrier = pltpu.get_barrier_semaphore()
@@ -58,48 +67,7 @@
                 device_id_type=pl.DeviceIdType.MESH,
             )
 
-    def arrival(c):
-        group = sum((c >= g * half).astype(jnp.int32) for g in range(1, groups))
-        within = c - group * half
-        k = sum((within >= i * step).astype(jnp.int32) for i in range(1, cuts))
-        return k * (groups - 1) * step + group * step + within
-
-    def iota(shape, axis):
-        return lax.broadcasted_iota(jnp.int32, shape, axis)
-
-    cols = cols_in[...]
-    cols_down = jnp.transpose(jnp.broadcast_to(cols, (n_blk, n_blk)))
-    from_place = arrival(iota((n_blk, n_blk), 0))
-    chained = (cols_down == cols) & (from_place < arrival(iota((n_blk, n_blk), 1)))
-    before = jnp.max(jnp.where(chained, from_place, -1), axis=0, keepdims=True)
-    final = jnp.broadcast_to(cols_down[:, :1], (n_blk, blocks)) == iota((n_blk, blocks), 1)
-    last = jnp.where(final, arrival(iota((n_blk, blocks), 0)), -1)
-    last = jnp.max(last, axis=0, keepdims=True)
-    meta_here[...] = jnp.zeros_like(meta_here)
-    meta_here[0:1, 0:n_blk] = rows_in[...]
-    meta_here[1:2, 0:n_blk] = jnp.where(before < 0, n_blk, before)
-    meta_here[2:3, 0:blocks] = jnp.where(last < 0, n_blk, last)
-
-    slot = iota((slots, rows), 0)
-    expert = sum((slot >= e * cap).astype(jnp.int32) for e in range(1, experts))
-    place_in = (slot - expert * cap).astype(F32)
-    earlier = (iota((rows, rows), 0) < iota((rows, rows), 1)).astype(F32).astype(BF16)
-    for m in range(micro):
-        named = [ids[m, j:j + 1, :] == expert for j in range(TOP)]
-        hit = functools.reduce(jnp.logical_or, named)
-        ahead = jnp.dot(
-            hit.astype(F32).astype(BF16), earlier, preferred_element_type=F32
-        )
-        fits = hit & (ahead == place_in)
-        amount = sum(jnp.where(named[j], mix[m, j:j + 1, :], 0.0) for j in range(TOP))
-        disp[m] = fits.astype(F32).astype(BF16)
-        comb[m] = jnp.transpose(jnp.where(fits, amount, 0.0))
-
     pl.semaphore_wait(barrier, sum(n - 1 for n in sizes.values()))
-    meta_own.start()
-
-    def token_copy(m):
-        return pltpu.make_async_copy(tokens.at[m], held.at[m], tok_sem.at[m])
 
     def hand_copy(m):
         return remote(
@@ -135,8 +103,6 @@
     order = [(a, k, by) for k in range(cuts) for a in range(3) for by in range(1, shards)]
 
     def start_weights():
-        for by in range(1, shards):
-            meta_over_shard(by).start()
         for a, k, by in order:
             over_shard(a, k, by).start()
 
@@ -183,6 +149,9 @@
     def lanes(r):
         return pl.ds(pl.multiple_of(r * blk, blk), blk)
 
+    def chunk_rows(e):
+        return pl.ds(pl.multiple_of(e * (cap * blocks), 16), cap * blocks)
+
     def strided(r):
         return pl.ds(r, slots, stride=blocks)
 
@@ -197,10 +166,11 @@
                 disp[m], normed[:, lanes(r)], preferred_element_type=F32
             )
 
-        for e in range(experts):
-            send[m, e] = wide[pl.ds(e * cap * blocks, cap * blocks), :].astype(BF16)
-        for by in far_first:
-            chunk_out(m, by).start()
+        for by in far_first + [0]:
+            e = peer("expert", by)
+            send[m, e] = wide[chunk_rows(e), :].astype(BF16)
+            if by > 0:
+                chunk_out(m, by).start()
         chunk_self(m).start()
 
     def segment(s, k):
@@ -219,11 +189,12 @@
             parts[s, at] = product + parts[s, meta_s[s, 1, c]]
 
     def expert_part(m, first):
-        for by in range(1, experts):
+        chunk_self(m).wait()
+        wide[chunk_rows(me_e), :] = recv[m, me_e].astype(F32)
+        for by in far_first:
             chunk_out(m, by).wait()
-        chunk_self(m).wait()
-        for e in range(experts):
-            wide[pl.ds(e * cap * blocks, cap * blocks), :] = recv[m, e].astype(F32)
+            e = peer("expert", experts - by)
+            wide[chunk_rows(e), :] = recv[m, e].astype(F32)
         if first:
             for copy in own:
                 copy.wait()
@@ -272,18 +243,20 @@
                 total = total + parts[s, meta_s[s, 2, j]]
             wide[strided(j), :] = total
 
-        for e in range(experts):
-            ret_send[m, e] = wide[pl.ds(e * cap * blocks, cap * blocks), :].astype(BF16)
+        for by in far_first + [0]:
+            e = peer("expert", by)
+            ret_send[m, e] = wide[chunk_rows(e), :].astype(BF16)
+            if by > 0:
+                chunk_back(m, by).start()
+        back_own(m).start()
+
+    def combine(m):
+        back_own(m).wait()
+        wide[chunk_rows(me_e), :] = ret_recv[m, me_e].astype(F32)
         for by in far_first:
-            chunk_back(m, by).start()
-        back_own(m).start()
-
-    def combine(m):
-        for by in range(1, experts):
             chunk_back(m, by).wait()
-        back_own(m).wait()
-        for e in range(experts):
-            wide[pl.ds(e * cap * blocks, cap * blocks), :] = ret_recv[m, e].astype(F32)
+            e = peer("expert", experts - by)
+            wide[chunk_rows(e), :] = ret_recv[m, e].astype(F32)
 
         @pl.loop(0, blocks, unroll=8)
         def _(r):
@@ -293,14 +266,55 @@
             )
             out[m, :, lanes(r)] = (held[m, :, lanes(r)].astype(F32) + mixed).astype(BF16)
 
+    @pl.when(me_l == 0)
+    def _():
+        start_weights()
+
+    def arrival(c):
+        group = sum((c >= g * half).astype(jnp.int32) for g in range(1, groups))
+        within = c - group * half
+        k = sum((within >= i * step).astype(jnp.int32) for i in range(1, cuts))
+        return k * (groups - 1) * step + group * step + within
+
+    def iota(shape, axis):
+        return lax.broadcasted_iota(jnp.int32, shape, axis)
+
+    cols = cols_in[...]
+    cols_down = jnp.transpose(jnp.broadcast_to(cols, (n_blk, n_blk)))
+    from_place = arrival(iota((n_blk, n_blk), 0))
+    chained = (cols_down == cols) & (from_place < arrival(iota((n_blk, n_blk), 1)))
+    before = jnp.max(jnp.where(chained, from_place, -1), axis=0, keepdims=True)
+    final = jnp.broadcast_to(cols_down[:, :1], (n_blk, blocks)) == iota((n_blk, blocks), 1)
+    last = jnp.where(final, arrival(iota((n_blk, blocks), 0)), -1)
+    last = jnp.max(last, axis=0, keepdims=True)
+    meta_here[...] = jnp.zeros_like(meta_here)
+    meta_here[0:1, 0:n_blk] = rows_in[...]
+    meta_here[1:2, 0:n_blk] = jnp.where(before < 0, n_blk, before)
+    meta_here[2:3, 0:blocks] = jnp.where(last < 0, n_blk, last)
+
+    slot = iota((slots, rows), 0)
+    expert = sum((slot >= e * cap).astype(jnp.int32) for e in range(1, experts))
+    place_in = (slot - expert * cap).astype(F32)
+    earlier = (iota((rows, rows), 0) < iota((rows, rows), 1)).astype(F32).astype(BF16)
+    for m in range(micro):
+        named = [ids[m, j:j + 1, :] == expert for j in range(TOP)]
+        hit = functools.reduce(jnp.logical_or, named)
+        ahead = jnp.dot(
+            hit.astype(F32).astype(BF16), earlier, preferred_element_type=F32
+        )
+        fits = hit & (ahead == place_in)
+        amount = sum(jnp.where(named[j], mix[m, j:j + 1, :], 0.0) for j in range(TOP))
+        disp[m] = fits.astype(F32).astype(BF16)
+        comb[m] = jnp.transpose(jnp.where(fits, amount, 0.0))
+
+    meta_own.start()
+    for by in range(1, shards):
+        meta_over_shard(by).start()
     for s in range(shards):
         parts[s, n_blk] = jnp.zeros_like(parts[s, n_blk])
 
     @pl.when(me_l == 0)
     def _():
-        for m in range(micro):
-            token_copy(m).start()
-        start_weights()
         for m in range(micro):
             token_copy(m).wait()
             dispatch(m)

time: 97.1 us -> 96.3 us (level)
  no operation moved by 1% of the time
where the time goes in v3:
time: 96.3 us; the launch traced here: 96.1 us
  Pallas kernels  94 us (98%)
  local copies, waits for them, and re-layouts  2.06 us (2%)
    pallas_call x1, Pallas kernels, body(): pl.pallas_call(functools.partial(layer_kernel, dims), out_shape=jax.Shape...  94 us
    unnamed x1, local copies, waits for them, and re-layouts  2.06 us

profile of v3, /device:TPU:17, one launch (start us, length us, event | category | flops | bytes accessed | tf_op | source)
XLA Modules:
  0.0 96.1 jit_solution(9269899588592380418)
XLA Ops:
  0.0 94.0 %shard_map.91 = bf16[2,32,6144]{2,1,0:T(8,128)(2,1)} custom-call(bf16[2,32,6144]{2,1,0:T(8,128)(2,1)} %tokens.1, f32[1,6144]{1,0:T(1,128)} %gain.1, s32[2,2,32]{2,1,0:T(2,128)} %bitcast.16, f32[2,2,32]{2,1,0:T(2,128)} %bitcast.17, bf16[32,128,128]{2,1,0:T(8,128)(2,1)} %bitcast.13, bf16[32,128,128]{2,1,0:T(8,128)(2,1)} %bitcast.14, ...), custom_call_target="tpu_custom_call" | custom-call | tf_op jit(solution)/shard_map/pallas_call | solution.py:383
  94.0 2.1 %copy.11 = bf16[1,2,32,6144]{3,2,1,0:T(8,128)(2,1)} copy(bf16[1,2,32,6144]{3,2,1,0:T(8,128)(2,1)} %bitcast.12) | data formatting | bytes 1572864
